TPU v7x, 256 devices: a whole 4x4x8 slice. The times are simulated.
256 devices in a mesh: tm: 16 (over z, core), trans: 16 (over y, x).
Axes of the slice: x: 4, y: 4, z: 8, core: 2. Of those that a mesh axis runs over, the one named last changes fastest.
Arguments:
- light_field: float32 [2, 256, 32, 1024], P(None, 'trans', 'tm'), may hold values from -6 to 6
- gas_density: float32 [256, 1024], replicated, may hold values from 0.5 to 2
- phase_x: float32 [256], replicated, may hold values from -3.140625 to 3.140625
- phase_y: float32 [1024], replicated, may hold values from -3.140625 to 3.140625
Outputs:
- light_out: float32 [2, 256, 32, 1024], P(None, 'trans', 'tm')
- electrons: float32 [256, 32, 1024], P('trans', 'tm')
All inputs are finite; a program needn't handle non-finite values.
Results may differ from a plain program's by a relative error of at most 0.0003.
Values sent between devices are 32-bit elements; how exact they have to be, the bound alone decides.
A program may use at most 64 MiB of HBM per device.

v0:
```python
import functools
import math

import jax
import jax.numpy as jnp
import numpy as np
from jax import lax
from jax.experimental import pallas as pl
from jax.experimental.pallas import tpu as pltpu
from jax.sharding import PartitionSpec as P

RATE_COEF = 1.8e-08
RECOMB = 0.02
KERR_COEF = 0.3
PLASMA = 4.0

N = 16
LANES = 128
HALF = 64
NX = 256
NY = 1024
RADIX = 8

F32 = jnp.float32
MESH = pl.DeviceIdType.MESH
ROOT_HALF = math.sqrt(0.5)


def tables():
    j = np.arange(NX)
    angle = 2.0 * np.pi * ((j[:, None] * j[None, :]) % NX) / NX
    table_x = np.concatenate([np.cos(angle), np.sin(angle)], axis=1)
    b = np.arange(LANES)
    angle = 2.0 * np.pi * ((b[:, None] * b[None, :]) % LANES) / LANES
    c, s = np.cos(angle), np.sin(angle)
    forward = np.block([[c, -s], [s, c]])
    backward = np.block([[c, s], [-s, c]])
    k = np.arange(RADIX)
    angle = 2.0 * np.pi * (k[:, None] * b[None, :]) / NY
    twist = np.stack([np.cos(angle), np.sin(angle)])
    spread = (b[None, :] % 16 == b[:, None] // RADIX).astype(np.float32)
    return [np.asarray(t, np.float32) for t in (table_x, forward, backward, twist, spread)]


def sincos(x):
    n = jnp.floor(x * (2.0 / math.pi) + 0.5)
    r = x - n * 1.5703125
    r = r - n * 4.837512969970703125e-4
    r = r - n * 7.54978995489188216e-8
    z = r * r
    s = r + r * z * (-1.6666654611e-1 + z * (8.3321608736e-3 + z * -1.9515295891e-4))
    c = 1.0 - 0.5 * z + z * z * (
        4.166664568298827e-2 + z * (-1.388731625493765e-3 + z * 2.443315711809948e-5)
    )
    q = n.astype(jnp.int32)
    odd = (q & 1) == 1
    sin = jnp.where(odd, c, s)
    cos = jnp.where(odd, s, c)
    sin = jnp.where((q & 2) == 2, -sin, sin)
    cos = jnp.where(((q + 1) & 2) == 2, -cos, cos)
    return sin, cos


def dot(a, b):
    return lax.dot_general(
        a,
        b,
        (((1,), (0,)), ((), ())),
        precision=lax.Precision.HIGHEST,
        preferred_element_type=F32,
    )


def cadd(a, b):
    return (a[0] + b[0], a[1] + b[1])


def csub(a, b):
    return (a[0] - b[0], a[1] - b[1])


def radix8(x, sign):
    def turn(v):
        return (-v[1], v[0]) if sign > 0 else (v[1], -v[0])

    def four(p, q, r, s):
        e0, e1, e2, e3 = cadd(p, r), csub(p, r), cadd(q, s), turn(csub(q, s))
        return cadd(e0, e2), cadd(e1, e3), csub(e0, e2), csub(e1, e3)

    e = four(x[0], x[2], x[4], x[6])
    o = four(x[1], x[3], x[5], x[7])
    t1, t3 = turn(o[1]), turn(o[3])
    w1 = ((o[1][0] + t1[0]) * ROOT_HALF, (o[1][1] + t1[1]) * ROOT_HALF)
    w3 = ((t3[0] - o[3][0]) * ROOT_HALF, (t3[1] - o[3][1]) * ROOT_HALF)
    o = (o[0], w1, turn(o[2]), w3)
    return [cadd(e[k], o[k]) for k in range(4)] + [csub(e[k], o[k]) for k in range(4)]


def kernel(
    field_hbm, dens_hbm, phx_hbm, phy_hbm, tx_hbm, wf_hbm, wb_hbm, tw_hbm, sp_hbm,
    out_hbm, ele_hbm,
    field, dens1, dens2, phx, phy, tx, wf, wb, tw, sp,
    stage, bmat, mmat, turns,
    send1, recv1, work, dec, src, inten,
    send2, recv2, send3, recv3, send4, recv4, send5, recv5, send6, recv6,
    out, ele,
    in_sems, send_sem, recv_sem, ein_sem, out_sems,
):
    tm = lax.axis_index("tm")
    trans = lax.axis_index("trans")
    low = lax.broadcasted_iota(jnp.int32, (8, LANES), 1) < HALF

    row0 = pl.multiple_of(trans * N, N)
    col0 = pl.multiple_of((trans // 2) * LANES, LANES)
    loads = [
        pltpu.make_async_copy(a, b, in_sems.at[i])
        for i, (a, b) in enumerate(
            [
                (field_hbm, field),
                (tw_hbm, tw),
                (wf_hbm, wf),
                (phy_hbm, phy),
                (sp_hbm, sp),
                (wb_hbm, wb),
                (phx_hbm, phx),
                (tx_hbm, tx),
                (dens_hbm.at[:, pl.ds(col0, LANES)], dens1),
                (dens_hbm.at[pl.ds(row0, N), :], dens2),
            ]
        )
    ]
    for load in loads:
        load.start()

    barrier = pltpu.get_barrier_semaphore()

    def greet(r, carry):
        pl.semaphore_signal(
            barrier, inc=1, device_id={"trans": lax.rem(trans + r, N)}, device_id_type=MESH
        )
        pl.semaphore_signal(
            barrier, inc=1, device_id={"tm": lax.rem(tm + r, N)}, device_id_type=MESH
        )
        return carry

    lax.fori_loop(1, N, greet, 0)

    def exchange(axis, me, src_ref, dst_ref, phase):
        def one(r, carry):
            peer = lax.rem(me + r, N)
            pltpu.make_async_remote_copy(
                src_ref=src_ref.at[peer],
                dst_ref=dst_ref.at[me],
                send_sem=send_sem.at[phase],
                recv_sem=recv_sem.at[phase],
                device_id={axis: peer},
                device_id_type=MESH,
            ).start()
            return carry

        lax.fori_loop(1, N, one, 0)
        dst_ref[me] = src_ref[me]

    def arrived(dst_ref, phase):
        part = dst_ref.at[pl.ds(0, N - 1)]
        pltpu.make_async_copy(part, part, recv_sem.at[phase]).wait()

    def left(src_ref, phase):
        part = src_ref.at[pl.ds(0, N - 1)]
        pltpu.make_async_copy(part, part, send_sem.at[phase]).wait()

    def spectral():
        freq = dot(stage[...], wf[...])
        for k in range(RADIX):
            rows = slice(32 * k, 32 * k + 32)
            re, im = freq[rows, :LANES], freq[rows, LANES:]
            pr, pi = turns[1, k : k + 1, :], turns[0, k : k + 1, :]
            stage[rows, :LANES] = re * pr - im * pi
            stage[rows, LANES:] = re * pi + im * pr
        stage[...] = dot(stage[...], wb[...])

    def forward(blocks, t, xh):
        for k, (re, im) in enumerate(radix8(blocks, -1)):
            rows = slice(32 * k + 16 * t + 8 * xh, 32 * k + 16 * t + 8 * xh + 8)
            c, s = tw[0, k : k + 1, :], tw[1, k : k + 1, :]
            stage[rows, :LANES] = re * c + im * s
            stage[rows, LANES:] = im * c - re * s

    def back(t, xh):
        parts = []
        for k in range(RADIX):
            rows = slice(32 * k + 16 * t + 8 * xh, 32 * k + 16 * t + 8 * xh + 8)
            re, im = stage[rows, :LANES], stage[rows, LANES:]
            c, s = tw[0, k : k + 1, :], tw[1, k : k + 1, :]
            parts.append((re * c - im * s, im * c + re * s))
        return radix8(parts, 1)

    def swap(v):
        return pltpu.roll(v, HALF, 1)

    loads[0].wait()
    loads[1].wait()
    for xh in range(2):
        for t in range(2):
            forward(
                [
                    tuple(field[c, pl.ds(128 * xh + 2 * a + t, 8, stride=16), :] for c in range(2))
                    for a in range(RADIX)
                ],
                t,
                xh,
            )
    for load in loads[2:6]:
        load.wait()
    lane = lax.broadcasted_iota(jnp.int32, (8, LANES), 1)
    sub = lax.broadcasted_iota(jnp.int32, (8, LANES), 0)
    picked = jnp.concatenate(
        [jnp.where(lane % RADIX == sub, phy[r : r + 1, :], 0.0) for r in range(RADIX)], axis=0
    )
    picked = dot(picked, sp[...])
    phase = jnp.zeros((8, LANES), F32)
    for r in range(RADIX):
        phase = jnp.where(lane // 16 == r, picked[8 * r : 8 * r + 8, :], phase)
    sin, cos = sincos(phase)
    turns[0] = sin * (1.0 / NY)
    turns[1] = cos * (1.0 / NY)
    spectral()
    for xh in range(2):
        rows = slice(8 * xh, 8 * xh + 8)
        first, second = back(0, xh), back(1, xh)
        for a in range(RADIX):
            for c in range(2):
                u, v = first[a][c], second[a][c]
                send1[2 * a, c, rows, :] = jnp.where(low, u, swap(v))
                send1[2 * a + 1, c, rows, :] = jnp.where(low, swap(u), v)

    pl.semaphore_wait(barrier, 2 * (N - 1))
    exchange("trans", trans, send1, recv1, 0)

    for load in loads[6:]:
        load.wait()
    sin, cos = sincos(phx[...])
    sin, cos = sin * (1.0 / NX), cos * (1.0 / NX)
    cx, sx = tx[:, :NX], tx[:, NX:]
    bmat[:NX, :] = cx * cos - sx * sin
    bmat[NX:, :] = cx * sin + sx * cos
    both = dot(bmat[...], tx[...])
    mmat[:NX, :] = both[:NX, :NX] + both[NX:, NX:]
    mmat[NX:, :] = both[NX:, :NX] - both[:NX, NX:]

    def along_x(re, im):
        both = dot(mmat[...], jnp.concatenate([re, im], axis=1))
        return both[:NX, :LANES] - both[NX:, LANES:], both[NX:, :LANES] + both[:NX, LANES:]

    def rates(re, im, dens):
        intensity = re * re + im * im
        power = intensity * intensity
        power = power * power
        power = power * power
        rate = RATE_COEF * power
        lost = rate + RECOMB
        decays = jnp.exp(-lost)
        source = (1.0 - decays) * dens * (rate / lost)
        return intensity, decays, source

    arrived(recv1, 0)
    re, im = along_x(
        recv1[:, 0].reshape(NX, LANES), recv1[:, 1].reshape(NX, LANES)
    )
    work[0] = re
    work[1] = im

    odd_slab = lax.rem(trans, 2) == 1
    for k in range(N):
        gains, adds = [], []
        for xh in range(2):
            rows = slice(16 * k + 8 * xh, 16 * k + 8 * xh + 8)
            dens = dens1[rows, :]
            turned = swap(dens)
            dens = jnp.where(low, jnp.where(odd_slab, turned, dens), jnp.where(odd_slab, dens, turned))
            intensity, decays, source = rates(work[0, rows, :], work[1, rows, :], dens)
            inten[rows, :] = intensity
            dec[rows, :] = decays
            src[rows, :] = source
            gains.append(decays * swap(decays))
            adds.append(decays * swap(source) + source)
        send2[k, 0] = jnp.where(low, gains[0], gains[1])
        send2[k, 1] = jnp.where(low, swap(adds[0]), adds[1])
    exchange("tm", tm, send2, recv2, 1)
    arrived(recv2, 1)

    def scan(from_ref, to_ref):
        entering = jnp.zeros((8, LANES), F32)
        for k in range(N):
            to_ref[k] = entering
            entering = from_ref[k, 0] * entering + from_ref[k, 1]

    scan(recv2, send3)
    exchange("tm", tm, send3, recv3, 2)
    arrived(recv3, 2)
    for k in range(N):
        packed = recv3[k]
        turned = swap(packed)
        for xh in range(2):
            rows = slice(16 * k + 8 * xh, 16 * k + 8 * xh + 8)
            entering = jnp.where(low, packed, turned) if xh == 0 else jnp.where(low, turned, packed)
            decays, source = dec[rows, :], src[rows, :]
            earlier = decays * entering + source
            electrons = decays * jnp.where(low, entering, swap(earlier)) + source
            sin, cos = sincos(KERR_COEF * inten[rows, :] - PLASMA * electrons)
            re, im = work[0, rows, :], work[1, rows, :]
            work[0, rows, :] = re * cos - im * sin
            work[1, rows, :] = re * sin + im * cos

    re, im = along_x(work[0], work[1])
    send4[:, 0] = re.reshape(N, 16, LANES)
    send4[:, 1] = im.reshape(N, 16, LANES)
    exchange("trans", trans, send4, recv4, 3)
    arrived(recv4, 3)

    for xh in range(2):
        rows = slice(8 * xh, 8 * xh + 8)
        pairs = [
            [(recv4[2 * a, c, rows, :], recv4[2 * a + 1, c, rows, :]) for c in range(2)]
            for a in range(RADIX)
        ]
        forward([tuple(jnp.where(low, u, swap(v)) for u, v in pair) for pair in pairs], 0, xh)
        forward([tuple(jnp.where(low, swap(u), v) for u, v in pair) for pair in pairs], 1, xh)
    spectral()
    for xh in range(2):
        rows = slice(8 * xh, 8 * xh + 8)
        blocks = [back(t, xh) for t in range(2)]
        for a in range(RADIX):
            k = 8 * xh + a
            dens = dens2[rows, LANES * a : LANES * (a + 1)]
            got = []
            for t in range(2):
                re, im = blocks[t][a]
                at = slice(16 * k + 8 * t, 16 * k + 8 * t + 8)
                work[0, at, :] = re
                work[1, at, :] = im
                intensity, decays, source = rates(re, im, dens)
                inten[at, :] = intensity
                dec[at, :] = decays
                src[at, :] = source
                got.append((decays, source))
            send5[k, 0] = got[0][0] * got[1][0]
            send5[k, 1] = got[1][0] * got[0][1] + got[1][1]
    exchange("tm", tm, send5, recv5, 4)
    arrived(recv5, 4)
    scan(recv5, send6)
    exchange("tm", tm, send6, recv6, 5)
    arrived(recv6, 5)
    for k in range(N):
        xh, a = divmod(k, RADIX)
        electrons = recv6[k]
        for t in range(2):
            at = slice(16 * k + 8 * t, 16 * k + 8 * t + 8)
            electrons = dec[at, :] * electrons + src[at, :]
            sin, cos = sincos(KERR_COEF * inten[at, :] - PLASMA * electrons)
            re, im = work[0, at, :], work[1, at, :]
            to = pl.ds(128 * xh + 2 * a + t, 8, stride=16)
            out[0, to, :] = re * cos - im * sin
            out[1, to, :] = re * sin + im * cos
            ele[to, :] = electrons

    stores = [
        pltpu.make_async_copy(out, out_hbm, out_sems.at[0]),
        pltpu.make_async_copy(ele, ele_hbm, out_sems.at[1]),
    ]
    for store in stores:
        store.start()
    for phase_index, ref in enumerate((send1, send2, send3, send4, send5, send6)):
        left(ref, phase_index)
    for store in stores:
        store.wait()


def local(light_field, gas_density, phase_x, phase_y):
    consts = tables()
    rows = light_field.reshape(2, 16, 2, RADIX, LANES).transpose(0, 1, 3, 2, 4).reshape(2, NX, LANES)
    vmem = lambda *shape: pltpu.VMEM(shape, F32)
    block = vmem(N, 2, 16, LANES)
    small = vmem(N, 2, 8, LANES)
    tiny = vmem(N, 8, LANES)
    out, ele = pl.pallas_call(
        kernel,
        out_shape=(
            jax.ShapeDtypeStruct((2, NX, LANES), F32),
            jax.ShapeDtypeStruct((NX, LANES), F32),
        ),
        in_specs=[pl.BlockSpec(memory_space=pl.ANY)] * 9,
        out_specs=(pl.BlockSpec(memory_space=pl.ANY),) * 2,
        scratch_shapes=[
            vmem(2, NX, LANES), vmem(NX, LANES), vmem(16, NY), vmem(1, NX), vmem(8, LANES),
            vmem(NX, 2 * NX), vmem(NX, NX), vmem(NX, NX), vmem(2, 8, LANES), vmem(LANES, LANES),
            vmem(NX, NX), vmem(2 * NX, NX), vmem(2 * NX, NX), vmem(2, 8, LANES),
            block, block, vmem(2, NX, LANES), vmem(NX, LANES), vmem(NX, LANES), vmem(NX, LANES),
            small, small, tiny, tiny, block, block, small, small, tiny, tiny,
            vmem(2, NX, LANES), vmem(NX, LANES),
            pltpu.SemaphoreType.DMA((10,)),
            pltpu.SemaphoreType.DMA((6,)),
            pltpu.SemaphoreType.DMA((6,)),
            pltpu.SemaphoreType.DMA((N,)),
            pltpu.SemaphoreType.DMA((2,)),
        ],
        compiler_params=pltpu.CompilerParams(
            collective_id=0, has_side_effects=True, vmem_limit_bytes=32 * 1024 * 1024
        ),
        name="split_step",
    )(rows, gas_density, phase_x.reshape(1, NX), phase_y.reshape(RADIX, LANES), *consts)
    out = out.reshape(2, 16, RADIX, 2, LANES).transpose(0, 1, 3, 2, 4).reshape(2, 16, 2, NY)
    ele = ele.reshape(16, RADIX, 2, LANES).transpose(0, 2, 1, 3).reshape(16, 2, NY)
    return out, ele


def solution(mesh):
    placed = (P(None, "trans", "tm", None), P(), P(), P())
    return jax.shard_map(
        local,
        mesh=mesh,
        in_specs=placed,
        out_specs=(P(None, "trans", "tm", None), P("trans", "tm", None)),
        check_vma=False,
    )
```

profile of v0, /device:TPU:1, one launch (start us, length us, event | category | flops | bytes accessed | tf_op | source)
XLA Modules:
  0.0 58.0 jit_solution(11754590742441094710)
XLA Ops:
  0.6 0.0 copy-start.6
  0.6 0.0 copy-start.8
  0.7 0.7 %copy-done.6 = f32[2,8,128]{2,1,0:T(8,128)S(1)} copy-done((f32[2,8,128]{2,1,0:T(8,128)S(1)}, f32[2,8,128]{2,1,0:T(8,128)}, u32[]{:S(2)}) %copy-start.6) | copy-done | bytes 8216
  1.3 0.0 copy-done.8
  1.3 0.0 copy-start
  1.3 1.2 %copy-done = f32[256,1024]{1,0:T(8,128)S(1)} copy-done((f32[256,1024]{1,0:T(8,128)S(1)}, f32[256,1024]{1,0:T(8,128)}, u32[]{:S(2)}) %copy-start) | copy-done | bytes 1048600
  2.6 0.0 copy-start.1
  2.6 1.0 %copy-done.1 = f32[256,512]{1,0:T(8,128)S(1)} copy-done((f32[256,512]{1,0:T(8,128)S(1)}, f32[256,512]{1,0:T(8,128)}, u32[]{:S(2)}) %copy-start.1) | copy-done | bytes 524312
  3.6 0.0 copy-start.2
  3.6 0.9 %copy-done.2 = f32[2,16,2,1024]{3,2,1,0:T(2,128)S(1)} copy-done((f32[2,16,2,1024]{3,2,1,0:T(2,128)S(1)}, f32[2,16,2,1024]{3,2,1,0:T(2,128)}, u32[]{:S(2)}) %copy-start.2) | copy-done | bytes 262168
  4.6 0.0 copy-start.3
  4.6 0.9 %copy-done.3 = f32[256,256]{1,0:T(8,128)S(1)} copy-done((f32[256,256]{1,0:T(8,128)S(1)}, f32[256,256]{1,0:T(8,128)}, u32[]{:S(2)}) %copy-start.3) | copy-done | bytes 262168
  5.5 0.0 copy-start.4
  5.5 0.9 %copy-done.4 = f32[256,256]{1,0:T(8,128)S(1)} copy-done((f32[256,256]{1,0:T(8,128)S(1)}, f32[256,256]{1,0:T(8,128)}, u32[]{:S(2)}) %copy-start.4) | copy-done | bytes 262168
  6.5 0.0 copy-start.5
  6.5 0.8 %copy-done.5 = f32[128,128]{1,0:T(8,128)S(1)} copy-done((f32[128,128]{1,0:T(8,128)S(1)}, f32[128,128]{1,0:T(8,128)}, u32[]{:S(2)}) %copy-start.5) | copy-done | bytes 65560
  7.3 0.0 copy-start.7
  7.3 0.7 %copy-done.7 = f32[1024]{0:T(1024)S(1)} copy-done((f32[1024]{0:T(1024)S(1)}, f32[1024]{0:T(1024)}, u32[]{:S(2)}) %copy-start.7) | copy-done | bytes 4120
  8.0 48.6 %split_step.1 = (f32[2,256,128]{2,1,0:T(8,128)S(1)}, f32[256,128]{1,0:T(8,128)S(1)}) custom-call(f32[2,256,128]{2,1,0:T(8,128)S(1)} %bitcast.17, f32[256,1024]{1,0:T(8,128)S(1)} %copy-done, f32[1,256]{1,0:T(1,128)S(1)} %bitcast.21, f32[8,128]{1,0:T(8,128)S(1)} %bitcast.20, f32[256,512]{1,0:T(8,128)S(1)} %copy-done.1, f32[256,256]{1,0:T(8,128)S(1)} %copy-done.4, ...), custom_call_target="tpu_custom_call" | custom-call | tf_op jit(solution)/shard_map/split_step/pallas_call | solution.py:386
  56.6 0.7 %copy.16 = f32[2,16,2,1024]{3,2,1,0:T(2,128)} copy(f32[2,16,2,1024]{3,2,1,0:T(2,128)S(1)} %bitcast.18) | data formatting | bytes 524288
  57.3 0.7 %copy.17 = f32[16,2,1024]{2,1,0:T(2,128)} copy(f32[16,2,1024]{2,1,0:T(2,128)S(1)} %bitcast.19) | data formatting | bytes 262144
Async XLA Ops:
  0.6 0.7 %copy-start.6 = (f32[2,8,128]{2,1,0:T(8,128)S(1)}, f32[2,8,128]{2,1,0:T(8,128)}, u32[]{:S(2)}) copy-start(f32[2,8,128]{2,1,0:T(8,128)} %constant.13.clone.tw_hbm) | copy-start | bytes 24580
  0.6 0.7 %copy-start.8 = (f32[256]{0:T(256)S(1)}, f32[256]{0:T(256)}, u32[]{:S(2)}) copy-start(f32[256]{0:T(256)} %param.11) | copy-start | bytes 3076
  1.3 1.2 %copy-start = (f32[256,1024]{1,0:T(8,128)S(1)}, f32[256,1024]{1,0:T(8,128)}, u32[]{:S(2)}) copy-start(f32[256,1024]{1,0:T(8,128)} %dens_hbm.1) | copy-start | bytes 3145732
  2.6 1.0 %copy-start.1 = (f32[256,512]{1,0:T(8,128)S(1)}, f32[256,512]{1,0:T(8,128)}, u32[]{:S(2)}) copy-start(f32[256,512]{1,0:T(8,128)} %constant.10.clone.tx_hbm) | copy-start | bytes 1572868
  3.6 0.9 %copy-start.2 = (f32[2,16,2,1024]{3,2,1,0:T(2,128)S(1)}, f32[2,16,2,1024]{3,2,1,0:T(2,128)}, u32[]{:S(2)}) copy-start(f32[2,16,2,1024]{3,2,1,0:T(2,128)} %param.9) | copy-start | bytes 786436
  4.6 0.9 %copy-start.3 = (f32[256,256]{1,0:T(8,128)S(1)}, f32[256,256]{1,0:T(8,128)}, u32[]{:S(2)}) copy-start(f32[256,256]{1,0:T(8,128)} %constant.12.clone.wb_hbm) | copy-start | bytes 786436
  5.5 0.9 %copy-start.4 = (f32[256,256]{1,0:T(8,128)S(1)}, f32[256,256]{1,0:T(8,128)}, u32[]{:S(2)}) copy-start(f32[256,256]{1,0:T(8,128)} %constant.11.clone.wf_hbm) | copy-start | bytes 786436
  6.5 0.8 %copy-start.5 = (f32[128,128]{1,0:T(8,128)S(1)}, f32[128,128]{1,0:T(8,128)}, u32[]{:S(2)}) copy-start(f32[128,128]{1,0:T(8,128)} %constant.14.clone.sp_hbm) | copy-start | bytes 196612
  7.3 0.7 %copy-start.7 = (f32[1024]{0:T(1024)S(1)}, f32[1024]{0:T(1024)}, u32[]{:S(2)}) copy-start(f32[1024]{0:T(1024)} %param.12) | copy-start | bytes 12292
where the time goes:
time: 58.3 us; the launch traced here: 58 us
  Pallas kernels  48.6 us (83%)
  local copies, waits for them, and re-layouts  8.69 us (15%)
  between operations  0.66 us (1%)
    pallas_call x1, Pallas kernels, local(): pl.pallas_call(kernel, out_shape=(jax.ShapeDtypeStruct((2, NX, LANES), F3...  48.6 us
    unnamed x20, local copies, waits for them, and re-layouts  8.69 us

commit v1 on v0

--- a/solution.py
+++ b/solution.py
@@ -405,7 +405,7 @@
             pltpu.SemaphoreType.DMA((2,)),
         ],
         compiler_params=pltpu.CompilerParams(
-            collective_id=0, has_side_effects=True, vmem_limit_bytes=32 * 1024 * 1024
+            collective_id=0, has_side_effects=True, vmem_limit_bytes=60 * 1024 * 1024
         ),
         name="split_step",
     )(rows, gas_density, phase_x.reshape(1, NX), phase_y.reshape(RADIX, LANES), *consts)

time: 58.3 us -> 52.5 us (0.901)
  local copies, waits for them, and re-layouts: 8.69 us -> 2.36 us
  Pallas kernels: 48.6 us -> 49.3 us
    unnamed x20 -> x4, local copies, waits for them, and re-layouts: 8.69 us -> 2.36 us
    pallas_call x1, Pallas kernels: 48.6 us -> 49.3 us  [local(): pl.pallas_call(kernel, out_shape=(jax.ShapeDtypeStruct((2, NX, LANES), F3...]
where the time goes in v1:
time: 52.5 us; the launch traced here: 52.3 us
  Pallas kernels  49.3 us (94%)
  local copies, waits for them, and re-layouts  2.36 us (4%)
  between operations  0.65 us (1%)
    pallas_call x1, Pallas kernels, local(): pl.pallas_call(kernel, out_shape=(jax.ShapeDtypeStruct((2, NX, LANES), F3...  49.3 us
    unnamed x4, local copies, waits for them, and re-layouts  2.36 us

profile of v1, /device:TPU:1, one launch (start us, length us, event | category | flops | bytes accessed | tf_op | source)
XLA Modules:
  0.0 52.3 jit_solution(14568191427277904114)
XLA Ops:
  0.6 49.3 %split_step.1 = (f32[2,256,128]{2,1,0:T(8,128)}, f32[256,128]{1,0:T(8,128)}) custom-call(f32[2,256,128]{2,1,0:T(8,128)} %bitcast.17, f32[256,1024]{1,0:T(8,128)} %dens_hbm.1, f32[1,256]{1,0:T(1,128)} %bitcast.21, f32[8,128]{1,0:T(8,128)} %bitcast.20, f32[256,512]{1,0:T(8,128)} %constant.10.clone.tx_hbm, f32[256,256]{1,0:T(8,128)} %constant.11.clone.wf_hbm, ...), custom_call_target="tpu_custom_call" | custom-call | tf_op jit(solution)/shard_map/split_step/pallas_call | solution.py:386
  50.0 0.0 copy-start
  50.0 1.7 %copy.16 = f32[2,16,2,1024]{3,2,1,0:T(2,128)} copy(f32[2,16,2,1024]{3,2,1,0:T(2,128)} %bitcast.18) | data formatting | bytes 524288
  51.7 0.0 copy-done
  51.7 0.7 %copy.17 = f32[16,2,1024]{2,1,0:T(2,128)} copy(f32[16,2,1024]{2,1,0:T(2,128)S(1)} %bitcast.19) | data formatting | bytes 262144
Async XLA Ops:
  50.0 1.7 %copy-start = (f32[256,128]{1,0:T(8,128)S(1)}, f32[256,128]{1,0:T(8,128)}, u32[]{:S(2)}) copy-start(f32[256,128]{1,0:T(8,128)} %get-tuple-element.5) | copy-start | bytes 393220

commit v2 on v1

v2 whole, which is shorter than its diff:
```python
import functools
import math

import jax
import jax.numpy as jnp
import numpy as np
from jax import lax
from jax.experimental import pallas as pl
from jax.experimental.pallas import tpu as pltpu
from jax.sharding import PartitionSpec as P

RATE_COEF = 1.8e-08
RECOMB = 0.02
KERR_COEF = 0.3
PLASMA = 4.0

N = 16
LANES = 128
GROUP = 4
TEAM = N * GROUP
NX = 256
NY = 1024
RADIX = 8

F32 = jnp.float32
MESH = pl.DeviceIdType.MESH
ROOT_HALF = math.sqrt(0.5)


def tables():
    j = np.arange(NX)
    angle = 2.0 * np.pi * ((j[:, None] * j[None, :]) % NX) / NX
    table_x = np.concatenate([np.cos(angle), np.sin(angle)], axis=1)
    b = np.arange(LANES)
    angle = 2.0 * np.pi * ((b[:, None] * b[None, :]) % LANES) / LANES
    c, s = np.cos(angle), np.sin(angle)
    forward = np.block([[c, -s], [s, c]])
    backward = np.block([[c, s], [-s, c]])
    k = np.arange(RADIX)
    angle = 2.0 * np.pi * (k[:, None] * b[None, :]) / NY
    twist = np.stack([np.cos(angle), np.sin(angle)])
    spread = (b[None, :] % 16 == b[:, None] // RADIX).astype(np.float32)
    return [np.asarray(t, np.float32) for t in (table_x, forward, backward, twist, spread)]


def sincos(x):
    n = jnp.floor(x * (2.0 / math.pi) + 0.5)
    r = x - n * 1.5703125
    r = r - n * 4.837512969970703125e-4
    r = r - n * 7.54978995489188216e-8
    z = r * r
    s = r + r * z * (-1.6666654611e-1 + z * (8.3321608736e-3 + z * -1.9515295891e-4))
    c = 1.0 - 0.5 * z + z * z * (
        4.166664568298827e-2 + z * (-1.388731625493765e-3 + z * 2.443315711809948e-5)
    )
    q = n.astype(jnp.int32)
    odd = (q & 1) == 1
    sin = jnp.where(odd, c, s)
    cos = jnp.where(odd, s, c)
    sin = jnp.where((q & 2) == 2, -sin, sin)
    cos = jnp.where(((q + 1) & 2) == 2, -cos, cos)
    return sin, cos


def dot(a, b):
    return lax.dot_general(
        a,
        b,
        (((1,), (0,)), ((), ())),
        precision=lax.Precision.HIGHEST,
        preferred_element_type=F32,
    )


def cadd(a, b):
    return (a[0] + b[0], a[1] + b[1])


def csub(a, b):
    return (a[0] - b[0], a[1] - b[1])


def radix8(x, sign):
    def turn(v):
        return (-v[1], v[0]) if sign > 0 else (v[1], -v[0])

    def four(p, q, r, s):
        e0, e1, e2, e3 = cadd(p, r), csub(p, r), cadd(q, s), turn(csub(q, s))
        return cadd(e0, e2), cadd(e1, e3), csub(e0, e2), csub(e1, e3)

    e = four(x[0], x[2], x[4], x[6])
    o = four(x[1], x[3], x[5], x[7])
    t1, t3 = turn(o[1]), turn(o[3])
    w1 = ((o[1][0] + t1[0]) * ROOT_HALF, (o[1][1] + t1[1]) * ROOT_HALF)
    w3 = ((t3[0] - o[3][0]) * ROOT_HALF, (t3[1] - o[3][1]) * ROOT_HALF)
    o = (o[0], w1, turn(o[2]), w3)
    return [cadd(e[k], o[k]) for k in range(4)] + [csub(e[k], o[k]) for k in range(4)]


def roll(v, by, axis):
    return pltpu.roll(v, by % v.shape[axis], axis)


def transpose_lanes(blocks, width):
    blocks = list(blocks)
    group = lax.broadcasted_iota(jnp.int32, (8, LANES), 1) // width
    bit = len(blocks) // 2
    while bit:
        clear = lax.rem(group // bit, 2) == 0
        for u in range(len(blocks)):
            if u & bit == 0:
                p, q = blocks[u], blocks[u | bit]
                blocks[u] = jnp.where(clear, p, roll(q, bit * width, 1))
                blocks[u | bit] = jnp.where(clear, roll(p, -bit * width, 1), q)
        bit //= 2
    return blocks


def spread_lanes(v):
    group = lax.broadcasted_iota(jnp.int32, (8, LANES), 1) // 16
    out = [v]
    for bit in (4, 2, 1):
        clear = lax.rem(group // bit, 2) == 0
        nxt = []
        for x in out:
            nxt.append(jnp.where(clear, x, roll(x, 16 * bit, 1)))
            nxt.append(jnp.where(clear, roll(x, -16 * bit, 1), x))
        out = nxt
    return out


def rates(re, im, dens):
    intensity = re * re + im * im
    power = intensity * intensity
    power = power * power
    power = power * power
    rate = RATE_COEF * power
    lost = rate + RECOMB
    decays = jnp.exp(-lost)
    source = (1.0 - decays) * dens * (rate / lost)
    return intensity, decays, source


def kernel(
    field_hbm, dens_hbm, phx_hbm, phy_hbm, tx_hbm, wf_hbm, wb_hbm, tw_hbm, sp_hbm,
    out, ele,
    field, dens1, dens2, phx, phy, tx, wf, wb, tw, sp,
    stage, bmat, mmat, mmix, turns, densx, densy,
    send1, recv1, work, gain, phase0,
    send2, recv2, ent, send4, recv4, fold, dec, src, inten,
    sende, recve, send5, recv5, ent5, send6, recv6,
    in_sems, ready, team_send, team_recv, map_send, map_recv, own_send, own_recv,
):
    tm = lax.axis_index("tm")
    trans = lax.axis_index("trans")
    g = tm // GROUP
    s = lax.rem(tm, GROUP)
    me = GROUP * trans + s

    barrier = pltpu.get_barrier_semaphore()

    def mate(r):
        other = lax.rem(trans + r // GROUP, N)
        slot = lax.rem(s + lax.rem(r, GROUP), GROUP)
        return (GROUP * g + slot, other), GROUP * other + slot

    def greet(r, carry):
        where_to, _ = mate(r)
        pl.semaphore_signal(barrier, inc=1, device_id=where_to, device_id_type=MESH)
        return carry

    row0 = pl.multiple_of(trans * N, N)
    col0 = pl.multiple_of((me // 8) * LANES, LANES)
    loads = [
        pltpu.make_async_copy(a, b, in_sems.at[i])
        for i, (a, b) in enumerate(
            [
                (field_hbm, field),
                (tw_hbm, tw),
                (wf_hbm, wf),
                (phy_hbm, phy),
                (sp_hbm, sp),
                (wb_hbm, wb),
                (phx_hbm, phx),
                (tx_hbm, tx),
                (dens_hbm.at[:, pl.ds(col0, LANES)], dens1),
                (dens_hbm.at[pl.ds(row0, N), :], dens2),
            ]
        )
    ]
    for load in loads:
        load.start()
    lax.fori_loop(1, TEAM, greet, 0)
    for later in range(1, GROUP):

        @pl.when(g + later < GROUP)
        def _():
            pl.semaphore_signal(
                barrier, inc=1, device_id=(tm + GROUP * later, trans), device_id_type=MESH
            )

    def exchange(src_ref, dst_ref, phase):
        def one(r, carry):
            where_to, slot = mate(r)
            pltpu.make_async_remote_copy(
                src_ref=src_ref.at[slot],
                dst_ref=dst_ref.at[me],
                send_sem=team_send.at[phase],
                recv_sem=team_recv.at[phase],
                device_id=where_to,
                device_id_type=MESH,
            ).start()
            return carry

        lax.fori_loop(1, TEAM, one, 0)
        dst_ref[me] = src_ref[me]

    def whole(ref, sem, count):
        part = ref.at[pl.ds(0, count)]
        pltpu.make_async_copy(part, part, sem).wait()

    def send_map(src_ref, dst_ref, phase, chunk):
        for later in range(1, GROUP):

            @pl.when(g + later < GROUP)
            def _():
                pltpu.make_async_remote_copy(
                    src_ref=src_ref.at[chunk],
                    dst_ref=dst_ref.at[g, chunk],
                    send_sem=map_send.at[phase],
                    recv_sem=map_recv.at[phase, g],
                    device_id=(tm + GROUP * later, trans),
                    device_id_type=MESH,
                ).start()

    def enter(dst_ref, phase, total):
        total[...] = jnp.zeros_like(total)
        for k in range(GROUP - 1):

            @pl.when(k < g)
            def _():
                pltpu.make_async_copy(dst_ref.at[k], dst_ref.at[k], map_recv.at[phase, k]).wait()
                for chunk in range(4):
                    total[chunk] = dst_ref[k, chunk, 0] * total[chunk] + dst_ref[k, chunk, 1]

    def send_own(src_ref, dst_ref, phase, i):
        @pl.when(i != s)
        def _():
            pltpu.make_async_remote_copy(
                src_ref=src_ref.at[i],
                dst_ref=dst_ref.at[s],
                send_sem=own_send.at[phase],
                recv_sem=own_recv.at[phase, s],
                device_id=(GROUP * g + i, trans),
                device_id_type=MESH,
            ).start()

    lane = lax.broadcasted_iota(jnp.int32, (8, LANES), 1)
    sub = lax.broadcasted_iota(jnp.int32, (8, LANES), 0)
    group = lane // 16
    top = sub < 4

    def flip(v):
        return roll(v, 4, 0)

    def spectral():
        freq = dot(stage[...], wf[...])
        for k in range(RADIX):
            rows = slice(32 * k, 32 * k + 32)
            re, im = freq[rows, :LANES], freq[rows, LANES:]
            pr, pi = turns[1, k : k + 1, :], turns[0, k : k + 1, :]
            stage[rows, :LANES] = re * pr - im * pi
            stage[rows, LANES:] = re * pi + im * pr
        stage[...] = dot(stage[...], wb[...])

    def forward(blocks, w):
        for k, (re, im) in enumerate(radix8(blocks, -1)):
            rows = slice(32 * k + 8 * w, 32 * k + 8 * w + 8)
            c, d = tw[0, k : k + 1, :], tw[1, k : k + 1, :]
            stage[rows, :LANES] = re * c + im * d
            stage[rows, LANES:] = im * c - re * d

    def back(w):
        parts = []
        for k in range(RADIX):
            rows = slice(32 * k + 8 * w, 32 * k + 8 * w + 8)
            re, im = stage[rows, :LANES], stage[rows, LANES:]
            c, d = tw[0, k : k + 1, :], tw[1, k : k + 1, :]
            parts.append((re * c - im * d, im * c + re * d))
        return radix8(parts, 1)

    loads[0].wait()
    loads[1].wait()
    for xh in range(2):
        for t in range(2):
            forward(
                [
                    tuple(field[c, pl.ds(128 * xh + 2 * a + t, 8, stride=16), :] for c in range(2))
                    for a in range(RADIX)
                ],
                2 * xh + t,
            )
    for load in loads[2:6]:
        load.wait()
    picked = jnp.concatenate(
        [jnp.where(lane % RADIX == sub, phy[r : r + 1, :], 0.0) for r in range(RADIX)], axis=0
    )
    picked = dot(picked, sp[...])
    phase = jnp.zeros((8, LANES), F32)
    for r in range(RADIX):
        phase = jnp.where(group == r, picked[8 * r : 8 * r + 8, :], phase)
    sin, cos = sincos(phase)
    turns[0] = sin * (1.0 / NY)
    turns[1] = cos * (1.0 / NY)
    spectral()
    parts = [back(w) for w in range(4)]
    for a in range(RADIX):
        mixed = transpose_lanes(
            [parts[2 * xh + t][a][c] for xh in range(2) for c in range(2) for t in range(2)], 16
        )
        for j in range(8):
            send1[8 * a + j] = mixed[j]

    pl.semaphore_wait(barrier, TEAM - 1 + g)
    exchange(send1, recv1, 0)
    for k in range(GROUP - 1):

        @pl.when(k < g)
        def _():
            pl.semaphore_signal(
                ready, inc=1, device_id=(GROUP * k + s, trans), device_id_type=MESH
            )

    for load in loads[6:]:
        load.wait()
    sin, cos = sincos(phx[...])
    sin, cos = sin * (1.0 / NX), cos * (1.0 / NX)
    cx, sx = tx[:, :NX], tx[:, NX:]
    bmat[:NX, :] = cx * cos - sx * sin
    bmat[NX:, :] = cx * sin + sx * cos
    both = dot(bmat[...], tx[...])
    mmat[:NX, :] = both[:NX, :NX] + both[NX:, NX:]
    mmat[NX:, :] = both[NX:, :NX] - both[:NX, NX:]
    for m in range(NX // 8):
        for half in range(2):
            cols = slice(LANES * half, LANES * (half + 1))
            re, im = mmat[8 * m : 8 * m + 8, cols], mmat[NX + 8 * m : NX + 8 * m + 8, cols]
            mmix[16 * m : 16 * m + 8, cols] = jnp.where(top, re, flip(im))
            mmix[16 * m + 8 : 16 * m + 16, cols] = jnp.where(top, flip(re), im)
    mine = group == lax.rem(me, 8)
    for m in range(NX // 8):
        rows = slice(8 * m, 8 * m + 8)
        v = jnp.where(mine, dens1[rows, :], 0.0)
        for shift in (16, 32, 64):
            v = v + roll(v, shift, 1)
        densx[rows, :] = v
    for r in range(4):
        line = dens2[pl.ds(4 * s + r, 1), :]
        densy[r : r + 1, :] = line
        densy[r + 4 : r + 5, :] = line

    whole(recv1, team_recv.at[0], TEAM - 1)
    for p in range(N):
        mixed = transpose_lanes([recv1[4 * p + k] for k in range(4)], 32)
        for xh in range(2):
            for c in range(2):
                work[c, 16 * p + 8 * xh : 16 * p + 8 * xh + 8, :] = mixed[2 * xh + c]
    both = dot(mmat[...], jnp.concatenate([work[0], work[1]], axis=1))
    work[0] = both[:NX, :LANES] - both[NX:, LANES:]
    work[1] = both[NX:, :LANES] + both[:NX, LANES:]

    @pl.when(g < GROUP - 1)
    def _():
        pl.semaphore_wait(ready, GROUP - 1 - g)

    for chunk in range(4):
        maps = [jnp.zeros((8, LANES), F32)] * 2
        for i in range(8):
            rows = slice(64 * chunk + 8 * i, 64 * chunk + 8 * i + 8)
            intensity, grow, add = rates(work[0, rows, :], work[1, rows, :], densx[rows, :])
            for bit in (1, 2, 4):
                there = group >= bit
                grow2, add2 = roll(grow, 16 * bit, 1), roll(add, 16 * bit, 1)
                add = jnp.where(there, grow * add2 + add, add)
                grow = jnp.where(there, grow * grow2, grow)
            phase0[rows, :] = KERR_COEF * intensity - PLASMA * add
            gain[rows, :] = PLASMA * grow
            maps = [
                jnp.where(group == i, roll(v, 16 * (i + 1), 1), old)
                for v, old in zip((grow, add), maps)
            ]
        send2[chunk, 0] = maps[0]
        send2[chunk, 1] = maps[1]
        send_map(send2, recv2, 0, chunk)
    enter(recv2, 0, ent)
    for chunk in range(4):
        for i, entering in enumerate(spread_lanes(ent[chunk])):
            rows = slice(64 * chunk + 8 * i, 64 * chunk + 8 * i + 8)
            sin, cos = sincos(phase0[rows, :] - gain[rows, :] * entering)
            re, im = work[0, rows, :], work[1, rows, :]
            work[0, rows, :] = re * cos - im * sin
            work[1, rows, :] = re * sin + im * cos

    both = dot(mmix[...], jnp.concatenate([work[0], work[1]], axis=1))
    for k in range(TEAM):
        rows = slice(8 * k, 8 * k + 8)
        turned = flip(both[rows, LANES:])
        send4[k] = both[rows, :LANES] + jnp.where(top, -turned, turned)
    exchange(send4, recv4, 1)
    whole(recv4, team_recv.at[1], TEAM - 1)

    for a in range(RADIX):
        times = transpose_lanes([recv4[8 * a + j] for j in range(8)], 16)
        for i in range(4):
            u, v = times[2 * i], times[2 * i + 1]
            fold[i, a, 0] = jnp.where(top, u, flip(v))
            fold[i, a, 1] = jnp.where(top, flip(u), v)
    for i in range(4):
        forward([(fold[i, a, 0], fold[i, a, 1]) for a in range(RADIX)], i)
    spectral()
    maps = [None] * 4
    for i in range(4):
        fields = back(i)
        pairs = []
        for a in range(RADIX):
            re, im = fields[a]
            sende[i, a, 0] = re
            sende[i, a, 1] = im
            _, decays, source = rates(re, im, densy[:, LANES * a : LANES * (a + 1)])
            dec[i, a] = decays
            src[i, a] = source
            pairs.append((decays * flip(decays), decays * flip(source) + source))
        for h in range(4):
            even, odd = pairs[2 * h], pairs[2 * h + 1]
            grow = jnp.where(top, even[0], odd[0])
            add = jnp.where(top, flip(even[1]), odd[1])
            if maps[h] is not None:
                grow, add = grow * maps[h][0], grow * maps[h][1] + add
            maps[h] = (grow, add)
    for h in range(4):
        send5[h, 0] = maps[h][0]
        send5[h, 1] = maps[h][1]
        send_map(send5, recv5, 1, h)
    for i in range(GROUP):
        send_own(sende, recve, 0, i)
    recve[s] = sende[s]

    enter(recv5, 1, ent5)
    current = []
    for h in range(4):
        v = ent5[h]
        turned = flip(v)
        current += [jnp.where(top, v, turned), jnp.where(top, turned, v)]
    for i in range(4):
        for a in range(RADIX):
            decays, source = dec[i, a], src[i, a]
            first = decays * current[a] + source
            electrons = decays * jnp.where(top, current[a], flip(first)) + source
            send6[i, a] = electrons
            current[a] = jnp.where(top, flip(electrons), electrons)
        send_own(send6, recv6, 1, i)
    recv6[s] = send6[s]

    for k in range(GROUP):

        @pl.when(k != s)
        def _():
            pltpu.make_async_copy(recve.at[k], recve.at[k], own_recv.at[0, k]).wait()
            pltpu.make_async_copy(recv6.at[k], recv6.at[k], own_recv.at[1, k]).wait()

        for a in range(RADIX):
            re, im, electrons = recve[k, a, 0], recve[k, a, 1], recv6[k, a]
            intensity = re * re + im * im
            sin, cos = sincos(KERR_COEF * intensity - PLASMA * electrons)
            new_re, new_im = re * cos - im * sin, re * sin + im * cos
            for t in range(2):
                rows = pl.ds(64 * k + 2 * a + t, 4, stride=16)
                part = slice(4 * t, 4 * t + 4)
                out[0, rows, :] = new_re[part]
                out[1, rows, :] = new_im[part]
                ele[rows, :] = electrons[part]

    whole(send1, team_send.at[0], TEAM - 1)
    whole(send4, team_send.at[1], TEAM - 1)
    whole(sende, own_send.at[0], GROUP - 1)
    whole(send6, own_send.at[1], GROUP - 1)
    for later in range(1, GROUP):

        @pl.when(g + later < GROUP)
        def _():
            for phase_index, ref in enumerate((send2, send5)):
                whole(ref, map_send.at[phase_index], 4)


def local(light_field, gas_density, phase_x, phase_y):
    consts = tables()
    rows = light_field.reshape(2, 16, 2, RADIX, LANES).transpose(0, 1, 3, 2, 4).reshape(2, NX, LANES)
    vmem = lambda *shape: pltpu.VMEM(shape, F32)
    team = vmem(TEAM, 8, LANES)
    chunks = vmem(4, 2, 8, LANES)
    incoming = vmem(GROUP - 1, 4, 2, 8, LANES)
    tall = vmem(4, RADIX, 8, LANES)
    fields = vmem(4, RADIX, 2, 8, LANES)
    plane = vmem(NX, LANES)
    out, ele = pl.pallas_call(
        kernel,
        out_shape=(
            jax.ShapeDtypeStruct((2, NX, LANES), F32),
            jax.ShapeDtypeStruct((NX, LANES), F32),
        ),
        in_specs=[pl.BlockSpec(memory_space=pltpu.HBM)] * 9,
        out_specs=(pl.BlockSpec(memory_space=pltpu.VMEM),) * 2,
        scratch_shapes=[
            vmem(2, NX, LANES), plane, vmem(16, NY), vmem(1, NX), vmem(8, LANES),
            vmem(NX, 2 * NX), vmem(NX, NX), vmem(NX, NX), vmem(2, 8, LANES), vmem(LANES, LANES),
            vmem(NX, NX), vmem(2 * NX, NX), vmem(2 * NX, NX), vmem(2 * NX, NX),
            vmem(2, 8, LANES), plane, vmem(8, NY),
            team, team, vmem(2, NX, LANES), plane, plane,
            chunks, incoming, vmem(4, 8, LANES), team, team, fields, tall, tall, tall,
            fields, fields, chunks, incoming, vmem(4, 8, LANES), tall, tall,
            pltpu.SemaphoreType.DMA((10,)),
            pltpu.SemaphoreType.REGULAR,
            pltpu.SemaphoreType.DMA((2,)),
            pltpu.SemaphoreType.DMA((2,)),
            pltpu.SemaphoreType.DMA((2,)),
            pltpu.SemaphoreType.DMA((2, GROUP - 1)),
            pltpu.SemaphoreType.DMA((2,)),
            pltpu.SemaphoreType.DMA((2, GROUP)),
        ],
        compiler_params=pltpu.CompilerParams(
            collective_id=0, has_side_effects=True, vmem_limit_bytes=60 * 1024 * 1024
        ),
        name="split_step",
    )(rows, gas_density, phase_x.reshape(1, NX), phase_y.reshape(RADIX, LANES), *consts)
    out = out.reshape(2, 16, RADIX, 2, LANES).transpose(0, 1, 3, 2, 4).reshape(2, 16, 2, NY)
    ele = ele.reshape(16, RADIX, 2, LANES).transpose(0, 2, 1, 3).reshape(16, 2, NY)
    return out, ele


def solution(mesh):
    placed = (P(None, "trans", "tm", None), P(), P(), P())
    return jax.shard_map(
        local,
        mesh=mesh,
        in_specs=placed,
        out_specs=(P(None, "trans", "tm", None), P("trans", "tm", None)),
        check_vma=False,
    )
```

time: 52.5 us -> 39.5 us (0.75)
  Pallas kernels: 49.3 us -> 35.8 us
    pallas_call x1, Pallas kernels: 49.3 us -> 35.8 us  [local(): pl.pallas_call(kernel, out_shape=(jax.ShapeDtypeStruct((2, NX, LANES), F3...]
where the time goes in v2:
time: 39.5 us; the launch traced here: 38.8 us
  Pallas kernels  35.8 us (91%)
  local copies, waits for them, and re-layouts  2.36 us (6%)
  between operations  0.65 us (2%)
    pallas_call x1, Pallas kernels, local(): pl.pallas_call(kernel, out_shape=(jax.ShapeDtypeStruct((2, NX, LANES), F3...  35.8 us
    unnamed x4, local copies, waits for them, and re-layouts  2.36 us

profile of v2, /device:TPU:1, one launch (start us, length us, event | category | flops | bytes accessed | tf_op | source)
XLA Modules:
  0.0 38.8 jit_solution(16708286060868842444)
XLA Ops:
  0.6 35.8 %split_step.1 = (f32[2,256,128]{2,1,0:T(8,128)}, f32[256,128]{1,0:T(8,128)}) custom-call(f32[2,256,128]{2,1,0:T(8,128)} %bitcast.17, f32[256,1024]{1,0:T(8,128)} %dens_hbm.1, f32[1,256]{1,0:T(1,128)} %bitcast.21, f32[8,128]{1,0:T(8,128)} %bitcast.20, f32[256,512]{1,0:T(8,128)} %constant.10.clone.tx_hbm, f32[256,256]{1,0:T(8,128)} %constant.11.clone.wf_hbm, ...), custom_call_target="tpu_custom_call" | custom-call | tf_op jit(solution)/shard_map/split_step/pallas_call | solution.py:505
  36.5 0.0 copy-start
  36.5 1.7 %copy.16 = f32[2,16,2,1024]{3,2,1,0:T(2,128)} copy(f32[2,16,2,1024]{3,2,1,0:T(2,128)} %bitcast.18) | data formatting | bytes 524288
  38.2 0.0 copy-done
  38.2 0.7 %copy.17 = f32[16,2,1024]{2,1,0:T(2,128)} copy(f32[16,2,1024]{2,1,0:T(2,128)S(1)} %bitcast.19) | data formatting | bytes 262144
Async XLA Ops:
  36.5 1.7 %copy-start = (f32[256,128]{1,0:T(8,128)S(1)}, f32[256,128]{1,0:T(8,128)}, u32[]{:S(2)}) copy-start(f32[256,128]{1,0:T(8,128)} %get-tuple-element.5) | copy-start | bytes 393220

commit v3 on v2

--- a/solution.py
+++ b/solution.py
@@ -528,10 +528,17 @@
             pltpu.SemaphoreType.DMA((2, GROUP)),
         ],
         compiler_params=pltpu.CompilerParams(
-            collective_id=0, has_side_effects=True, vmem_limit_bytes=60 * 1024 * 1024
+            collective_id=0, has_side_effects=True, vmem_limit_bytes=24 * 1024 * 1024
         ),
         name="split_step",
-    )(rows, gas_density, phase_x.reshape(1, NX), phase_y.reshape(RADIX, LANES), *consts)
+    )(
+        *(
+            pltpu.with_memory_space_constraint(array, pltpu.HBM)
+            for array in (
+                rows, gas_density, phase_x.reshape(1, NX), phase_y.reshape(RADIX, LANES), *consts
+            )
+        )
+    )
     out = out.reshape(2, 16, RADIX, 2, LANES).transpose(0, 1, 3, 2, 4).reshape(2, 16, 2, NY)
     ele = ele.reshape(16, RADIX, 2, LANES).transpose(0, 2, 1, 3).reshape(16, 2, NY)
     return out, ele

time: 39.5 us -> 37.7 us (0.954)
  local copies, waits for them, and re-layouts: 2.36 us -> 1.36 us
  Pallas kernels: 35.8 us -> 35.1 us
    unnamed x4 -> x2, local copies, waits for them, and re-layouts: 2.36 us -> 1.36 us
    pallas_call x1, Pallas kernels: 35.8 us -> 35.1 us  [local(): pl.pallas_call(kernel, out_shape=(jax.ShapeDtypeStruct((2, NX, LANES), F3...]
where the time goes in v3:
time: 37.7 us; the launch traced here: 37.1 us
  Pallas kernels  35.1 us (93%)
  local copies, waits for them, and re-layouts  1.36 us (4%)
  between operations  0.64 us (2%)
    pallas_call x1, Pallas kernels, local(): pl.pallas_call(kernel, out_shape=(jax.ShapeDtypeStruct((2, NX, LANES), F3...  35.1 us
    unnamed x2, local copies, waits for them, and re-layouts  1.36 us

profile of v3, /device:TPU:1, one launch (start us, length us, event | category | flops | bytes accessed | tf_op | source)
XLA Modules:
  0.0 37.1 jit_solution(11974866274238725427)
XLA Ops:
  0.6 35.1 %split_step.1 = (f32[2,256,128]{2,1,0:T(8,128)S(1)}, f32[256,128]{1,0:T(8,128)S(1)}) custom-call(f32[2,256,128]{2,1,0:T(8,128)} %bitcast.19, f32[256,1024]{1,0:T(8,128)} %dens_hbm.1, f32[1,256]{1,0:T(1,128)} %bitcast.21, f32[8,128]{1,0:T(8,128)} %bitcast.20, f32[256,512]{1,0:T(8,128)} %constant.10.clone.tx_hbm, f32[256,256]{1,0:T(8,128)} %constant.11.clone.wf_hbm, ...), custom_call_target="tpu_custom_call" | custom-call | tf_op jit(solution)/shard_map/split_step/pallas_call | solution.py:505
  35.7 0.7 %copy.16 = f32[2,16,2,1024]{3,2,1,0:T(2,128)} copy(f32[2,16,2,1024]{3,2,1,0:T(2,128)S(1)} %bitcast.17) | data formatting | bytes 524288
  36.4 0.7 %copy.17 = f32[16,2,1024]{2,1,0:T(2,128)} copy(f32[16,2,1024]{2,1,0:T(2,128)S(1)} %bitcast.18) | data formatting | bytes 262144

commit v4 on v3

--- a/solution.py
+++ b/solution.py
@@ -25,6 +25,19 @@
 F32 = jnp.float32
 MESH = pl.DeviceIdType.MESH
 ROOT_HALF = math.sqrt(0.5)
+
+
+FAR_FIRST = sorted(
+    (
+        (dy, dx, dz, dc)
+        for dy in range(4)
+        for dx in range(4)
+        for dz in range(2)
+        for dc in range(2)
+        if dy or dx or dz or dc
+    ),
+    key=lambda d: -(min(d[0], 4 - d[0]) + min(d[1], 4 - d[1]) + d[2]) - 0.1 * d[3],
+)
 
 
 def tables():
@@ -159,15 +172,14 @@
 
     barrier = pltpu.get_barrier_semaphore()
 
-    def mate(r):
-        other = lax.rem(trans + r // GROUP, N)
-        slot = lax.rem(s + lax.rem(r, GROUP), GROUP)
-        return (GROUP * g + slot, other), GROUP * other + slot
-
-    def greet(r, carry):
-        where_to, _ = mate(r)
-        pl.semaphore_signal(barrier, inc=1, device_id=where_to, device_id_type=MESH)
-        return carry
+    ys = [GROUP * lax.rem(trans // 4 + d, 4) for d in range(4)]
+    xs = [lax.rem(trans + d, 4) for d in range(4)]
+    zs = [2 * lax.rem(s // 2 + d, 2) for d in range(2)]
+    cs = [lax.rem(s + d, 2) for d in range(2)]
+    mates = []
+    for dy, dx, dz, dc in FAR_FIRST:
+        other, slot = ys[dy] + xs[dx], zs[dz] + cs[dc]
+        mates.append(((GROUP * g + slot, other), GROUP * other + slot))
 
     row0 = pl.multiple_of(trans * N, N)
     col0 = pl.multiple_of((me // 8) * LANES, LANES)
@@ -188,9 +200,12 @@
             ]
         )
     ]
-    for load in loads:
+    for load in loads[:3]:
         load.start()
-    lax.fori_loop(1, TEAM, greet, 0)
+    for where_to, _ in mates:
+        pl.semaphore_signal(barrier, inc=1, device_id=where_to, device_id_type=MESH)
+    for load in loads[3:]:
+        load.start()
     for later in range(1, GROUP):
 
         @pl.when(g + later < GROUP)
@@ -200,8 +215,7 @@
             )
 
     def exchange(src_ref, dst_ref, phase):
-        def one(r, carry):
-            where_to, slot = mate(r)
+        for where_to, slot in mates:
             pltpu.make_async_remote_copy(
                 src_ref=src_ref.at[slot],
                 dst_ref=dst_ref.at[me],
@@ -210,9 +224,6 @@
                 device_id=where_to,
                 device_id_type=MESH,
             ).start()
-            return carry
-
-        lax.fori_loop(1, TEAM, one, 0)
         dst_ref[me] = src_ref[me]
 
     def whole(ref, sem, count):
@@ -490,6 +501,16 @@
         def _():
             for phase_index, ref in enumerate((send2, send5)):
                 whole(ref, map_send.at[phase_index], 4)
+
+
+def finish(a, b, c, d, sems):
+    copies = [
+        pltpu.make_async_copy(x, y, sems.at[i]) for i, (x, y) in enumerate([(a, c), (b, d)])
+    ]
+    for copy in copies:
+        copy.start()
+    for copy in copies:
+        copy.wait()
 
 
 def local(light_field, gas_density, phase_x, phase_y):
@@ -539,6 +560,18 @@
             )
         )
     )
+    out, ele = pl.pallas_call(
+        finish,
+        out_shape=(
+            jax.ShapeDtypeStruct((2, NX, LANES), F32),
+            jax.ShapeDtypeStruct((NX, LANES), F32),
+        ),
+        in_specs=[pl.BlockSpec(memory_space=pltpu.VMEM)] * 2,
+        out_specs=(pl.BlockSpec(memory_space=pltpu.HBM),) * 2,
+        scratch_shapes=[pltpu.SemaphoreType.DMA((2,))],
+        compiler_params=pltpu.CompilerParams(vmem_limit_bytes=1024 * 1024),
+        name="finish",
+    )(out, ele)
     out = out.reshape(2, 16, RADIX, 2, LANES).transpose(0, 1, 3, 2, 4).reshape(2, 16, 2, NY)
     ele = ele.reshape(16, RADIX, 2, LANES).transpose(0, 2, 1, 3).reshape(16, 2, NY)
     return out, ele

time: 37.7 us -> 35.4 us (0.939); the launches traced: 37.1 us -> 35.2 us
  local copies, waits for them, and re-layouts: 1.36 us -> 0 us
  Pallas kernels: 35.1 us -> 34.6 us
    unnamed x2 -> x0, local copies, waits for them, and re-layouts: 1.36 us -> none
    pallas_call x1, Pallas kernels: 35.1 us -> 33.8 us  [local(): pl.pallas_call(kernel, out_shape=(jax.ShapeDtypeStruct((2, NX, LANES), F3...]
    pallas_call x0 -> x1, Pallas kernels: none -> 0.76 us  [local(): pl.pallas_call(finish, out_shape=(jax.ShapeDtypeStruct((2, NX, LANES), F3...]
where the time goes in v4:
time: 35.4 us; the launch traced here: 35.2 us
  Pallas kernels  34.6 us (98%)
  between operations  0.64 us (2%)
    pallas_call x1, Pallas kernels, local(): pl.pallas_call(kernel, out_shape=(jax.ShapeDtypeStruct((2, NX, LANES), F3...  33.8 us
    pallas_call x1, Pallas kernels, local(): pl.pallas_call(finish, out_shape=(jax.ShapeDtypeStruct((2, NX, LANES), F3...  0.76 us

profile of v4, /device:TPU:1, one launch (start us, length us, event | category | flops | bytes accessed | tf_op | source)
XLA Modules:
  0.0 35.2 jit_solution(16930163772801731132)
XLA Ops:
  0.6 33.8 %split_step.1 = (f32[2,256,128]{2,1,0:T(8,128)S(1)}, f32[256,128]{1,0:T(8,128)S(1)}) custom-call(f32[2,256,128]{2,1,0:T(8,128)} %bitcast.17, f32[256,1024]{1,0:T(8,128)} %dens_hbm.1, f32[1,256]{1,0:T(1,128)} %bitcast.19, f32[8,128]{1,0:T(8,128)} %bitcast.18, f32[256,512]{1,0:T(8,128)} %constant.10.clone.tx_hbm, f32[256,256]{1,0:T(8,128)} %constant.11.clone.wf_hbm, ...), custom_call_target="tpu_custom_call" | custom-call | tf_op jit(solution)/shard_map/split_step/pallas_call | solution.py:526
  34.5 0.8 %finish.1 = (f32[2,256,128]{2,1,0:T(8,128)}, f32[256,128]{1,0:T(8,128)}) custom-call(f32[2,256,128]{2,1,0:T(8,128)S(1)} %get-tuple-element.6.a, f32[256,128]{1,0:T(8,128)S(1)} %get-tuple-element.7.b), custom_call_target="tpu_custom_call" | custom-call | tf_op jit(solution)/shard_map/finish/pallas_call | solution.py:563

commit v5 on v4

--- a/solution.py
+++ b/solution.py
@@ -38,6 +38,8 @@
     ),
     key=lambda d: -(min(d[0], 4 - d[0]) + min(d[1], 4 - d[1]) + d[2]) - 0.1 * d[3],
 )
+
+NEARNESS = ((2,), (1,), (3,), (0,))
 
 
 def tables():
@@ -85,6 +87,25 @@
     )
 
 
+def split(v, parts):
+    out = []
+    for _ in range(parts):
+        out.append(v.astype(jnp.bfloat16))
+        v = v - out[-1].astype(F32)
+    return out
+
+
+def dot_parts(a, b):
+    total = None
+    for order in range(len(a) - 1, -1, -1):
+        for i in range(order + 1):
+            term = lax.dot_general(
+                a[i], b[order - i], (((1,), (0,)), ((), ())), preferred_element_type=F32
+            )
+            total = term if total is None else total + term
+    return total
+
+
 def cadd(a, b):
     return (a[0] + b[0], a[1] + b[1])
 
@@ -159,7 +180,7 @@
     out, ele,
     field, dens1, dens2, phx, phy, tx, wf, wb, tw, sp,
     stage, bmat, mmat, mmix, turns, densx, densy,
-    send1, recv1, work, gain, phase0,
+    mparts, xparts, wparts, send1, recv1, work, gain, phase0,
     send2, recv2, ent, send4, recv4, fold, dec, src, inten,
     sende, recve, send5, recv5, ent5, send6, recv6,
     in_sems, ready, team_send, team_recv, map_send, map_recv, own_send, own_recv,
@@ -214,8 +235,10 @@
                 barrier, inc=1, device_id=(tm + GROUP * later, trans), device_id_type=MESH
             )
 
-    def exchange(src_ref, dst_ref, phase):
-        for where_to, slot in mates:
+    def exchange(src_ref, dst_ref, phase, near):
+        for offsets, (where_to, slot) in zip(FAR_FIRST, mates):
+            if offsets[0] not in near:
+                continue
             pltpu.make_async_remote_copy(
                 src_ref=src_ref.at[slot],
                 dst_ref=dst_ref.at[me],
@@ -224,7 +247,6 @@
                 device_id=where_to,
                 device_id_type=MESH,
             ).start()
-        dst_ref[me] = src_ref[me]
 
     def whole(ref, sem, count):
         part = ref.at[pl.ds(0, count)]
@@ -274,15 +296,15 @@
     def flip(v):
         return roll(v, 4, 0)
 
-    def spectral():
-        freq = dot(stage[...], wf[...])
+    def spectral(ahead, behind):
+        freq = ahead(stage[...])
         for k in range(RADIX):
             rows = slice(32 * k, 32 * k + 32)
             re, im = freq[rows, :LANES], freq[rows, LANES:]
             pr, pi = turns[1, k : k + 1, :], turns[0, k : k + 1, :]
             stage[rows, :LANES] = re * pr - im * pi
             stage[rows, LANES:] = re * pi + im * pr
-        stage[...] = dot(stage[...], wb[...])
+        stage[...] = behind(stage[...])
 
     def forward(blocks, w):
         for k, (re, im) in enumerate(radix8(blocks, -1)):
@@ -323,7 +345,7 @@
     sin, cos = sincos(phase)
     turns[0] = sin * (1.0 / NY)
     turns[1] = cos * (1.0 / NY)
-    spectral()
+    spectral(lambda v: dot(v, wf[...]), lambda v: dot(v, wb[...]))
     parts = [back(w) for w in range(4)]
     for a in range(RADIX):
         mixed = transpose_lanes(
@@ -333,7 +355,8 @@
             send1[8 * a + j] = mixed[j]
 
     pl.semaphore_wait(barrier, TEAM - 1 + g)
-    exchange(send1, recv1, 0)
+    exchange(send1, recv1, 0, range(4))
+    recv1[me] = send1[me]
     for k in range(GROUP - 1):
 
         @pl.when(k < g)
@@ -358,6 +381,14 @@
             re, im = mmat[8 * m : 8 * m + 8, cols], mmat[NX + 8 * m : NX + 8 * m + 8, cols]
             mmix[16 * m : 16 * m + 8, cols] = jnp.where(top, re, flip(im))
             mmix[16 * m + 8 : 16 * m + 16, cols] = jnp.where(top, flip(re), im)
+    for target, parts in (
+        (mparts, split(mmat[...], 3)),
+        (xparts, split(mmix[...], 2)),
+        (wparts.at[0], split(wf[...], 2)),
+        (wparts.at[1], split(wb[...], 2)),
+    ):
+        for i, part in enumerate(parts):
+            target[i] = part
     mine = group == lax.rem(me, 8)
     for m in range(NX // 8):
         rows = slice(8 * m, 8 * m + 8)
@@ -376,7 +407,9 @@
         for xh in range(2):
             for c in range(2):
                 work[c, 16 * p + 8 * xh : 16 * p + 8 * xh + 8, :] = mixed[2 * xh + c]
-    both = dot(mmat[...], jnp.concatenate([work[0], work[1]], axis=1))
+    both = dot_parts(
+        [mparts[i] for i in range(3)], split(jnp.concatenate([work[0], work[1]], axis=1), 3)
+    )
     work[0] = both[:NX, :LANES] - both[NX:, LANES:]
     work[1] = both[NX:, :LANES] + both[:NX, LANES:]
 
@@ -412,12 +445,28 @@
             work[0, rows, :] = re * cos - im * sin
             work[1, rows, :] = re * sin + im * cos
 
-    both = dot(mmix[...], jnp.concatenate([work[0], work[1]], axis=1))
-    for k in range(TEAM):
-        rows = slice(8 * k, 8 * k + 8)
-        turned = flip(both[rows, LANES:])
-        send4[k] = both[rows, :LANES] + jnp.where(top, -turned, turned)
-    exchange(send4, recv4, 1)
+    fields = split(jnp.concatenate([work[0], work[1]], axis=1), 2)
+    for near in NEARNESS:
+        both = dot_parts(
+            [
+                jnp.concatenate(
+                    [
+                        xparts[i, pl.ds(pl.multiple_of(32 * ys[dy], 128), 128), :]
+                        for dy in near
+                    ],
+                    axis=0,
+                )
+                for i in range(2)
+            ],
+            fields,
+        )
+        for n, dy in enumerate(near):
+            for k in range(16):
+                rows = slice(128 * n + 8 * k, 128 * n + 8 * k + 8)
+                turned = flip(both[rows, LANES:])
+                send4[GROUP * ys[dy] + k] = both[rows, :LANES] + jnp.where(top, -turned, turned)
+        exchange(send4, recv4, 1, near)
+    recv4[me] = send4[me]
     whole(recv4, team_recv.at[1], TEAM - 1)
 
     for a in range(RADIX):
@@ -428,7 +477,9 @@
             fold[i, a, 1] = jnp.where(top, flip(u), v)
     for i in range(4):
         forward([(fold[i, a, 0], fold[i, a, 1]) for a in range(RADIX)], i)
-    spectral()
+    spectral(
+        *(lambda v, i=i: dot_parts(split(v, 2), [wparts[i, 0], wparts[i, 1]]) for i in range(2))
+    )
     maps = [None] * 4
     for i in range(4):
         fields = back(i)
@@ -536,6 +587,9 @@
             vmem(NX, 2 * NX), vmem(NX, NX), vmem(NX, NX), vmem(2, 8, LANES), vmem(LANES, LANES),
             vmem(NX, NX), vmem(2 * NX, NX), vmem(2 * NX, NX), vmem(2 * NX, NX),
             vmem(2, 8, LANES), plane, vmem(8, NY),
+            pltpu.VMEM((3, 2 * NX, NX), jnp.bfloat16),
+            pltpu.VMEM((2, 2 * NX, NX), jnp.bfloat16),
+            pltpu.VMEM((2, 2, NX, NX), jnp.bfloat16),
             team, team, vmem(2, NX, LANES), plane, plane,
             chunks, incoming, vmem(4, 8, LANES), team, team, fields, tall, tall, tall,
             fields, fields, chunks, incoming, vmem(4, 8, LANES), tall, tall,

time: 35.4 us -> 34.1 us (0.963)
  Pallas kernels: 34.6 us -> 33.4 us
    pallas_call x1, Pallas kernels: 33.8 us -> 32.6 us  [local(): pl.pallas_call(kernel, out_shape=(jax.ShapeDtypeStruct((2, NX, LANES), F3...]
where the time goes in v5:
time: 34.1 us; the launch traced here: 34 us
  Pallas kernels  33.4 us (98%)
  between operations  0.64 us (2%)
    pallas_call x1, Pallas kernels, local(): pl.pallas_call(kernel, out_shape=(jax.ShapeDtypeStruct((2, NX, LANES), F3...  32.6 us
    pallas_call x1, Pallas kernels, local(): pl.pallas_call(finish, out_shape=(jax.ShapeDtypeStruct((2, NX, LANES), F3...  0.76 us

profile of v5, /device:TPU:1, one launch (start us, length us, event | category | flops | bytes accessed | tf_op | source)
XLA Modules:
  0.0 34.0 jit_solution(4555447136001278174)
XLA Ops:
  0.6 32.6 %split_step.1 = (f32[2,256,128]{2,1,0:T(8,128)S(1)}, f32[256,128]{1,0:T(8,128)S(1)}) custom-call(f32[2,256,128]{2,1,0:T(8,128)} %bitcast.17, f32[256,1024]{1,0:T(8,128)} %dens_hbm.1, f32[1,256]{1,0:T(1,128)} %bitcast.19, f32[8,128]{1,0:T(8,128)} %bitcast.18, f32[256,512]{1,0:T(8,128)} %constant.10.clone.tx_hbm, f32[256,256]{1,0:T(8,128)} %constant.11.clone.wf_hbm, ...), custom_call_target="tpu_custom_call" | custom-call | tf_op jit(solution)/shard_map/split_step/pallas_call | solution.py:577
  33.2 0.8 %finish.1 = (f32[2,256,128]{2,1,0:T(8,128)}, f32[256,128]{1,0:T(8,128)}) custom-call(f32[2,256,128]{2,1,0:T(8,128)S(1)} %get-tuple-element.6.a, f32[256,128]{1,0:T(8,128)S(1)} %get-tuple-element.7.b), custom_call_target="tpu_custom_call" | custom-call | tf_op jit(solution)/shard_map/finish/pallas_call | solution.py:617

commit v6 on v5

--- a/solution.py
+++ b/solution.py
@@ -182,7 +182,7 @@
     stage, bmat, mmat, mmix, turns, densx, densy,
     mparts, xparts, wparts, send1, recv1, work, gain, phase0,
     send2, recv2, ent, send4, recv4, fold, dec, src, inten,
-    sende, recve, send5, recv5, ent5, send6, recv6,
+    sende, recve, send5, recv5, ent5, send6, recv6, pairmap,
     in_sems, ready, team_send, team_recv, map_send, map_recv, own_send, own_recv,
 ):
     tm = lax.axis_index("tm")
@@ -396,10 +396,11 @@
         for shift in (16, 32, 64):
             v = v + roll(v, shift, 1)
         densx[rows, :] = v
-    for r in range(4):
-        line = dens2[pl.ds(4 * s + r, 1), :]
-        densy[r : r + 1, :] = line
-        densy[r + 4 : r + 5, :] = line
+    for k in range(GROUP):
+        for r in range(4):
+            line = dens2[4 * k + r : 4 * k + r + 1, :]
+            densy[k, r : r + 1, :] = line
+            densy[k, r + 4 : r + 5, :] = line
 
     whole(recv1, team_recv.at[0], TEAM - 1)
     for p in range(N):
@@ -407,21 +408,32 @@
         for xh in range(2):
             for c in range(2):
                 work[c, 16 * p + 8 * xh : 16 * p + 8 * xh + 8, :] = mixed[2 * xh + c]
-    both = dot_parts(
-        [mparts[i] for i in range(3)], split(jnp.concatenate([work[0], work[1]], axis=1), 3)
-    )
-    work[0] = both[:NX, :LANES] - both[NX:, LANES:]
-    work[1] = both[NX:, :LANES] + both[:NX, LANES:]
-
-    @pl.when(g < GROUP - 1)
-    def _():
-        pl.semaphore_wait(ready, GROUP - 1 - g)
-
+    fields = split(jnp.concatenate([work[0], work[1]], axis=1), 3)
+
+    def along_x(chunk):
+        both = dot_parts(
+            [
+                jnp.concatenate(
+                    [mparts[i, n + 64 * chunk : n + 64 * chunk + 64, :] for n in (0, NX)], axis=0
+                )
+                for i in range(3)
+            ],
+            fields,
+        )
+        return both[:64, :LANES] - both[64:, LANES:], both[64:, :LANES] + both[:64, LANES:]
+
+    ahead = along_x(0)
     for chunk in range(4):
         maps = [jnp.zeros((8, LANES), F32)] * 2
+        re, im = ahead
+        if chunk < 3:
+            ahead = along_x(chunk + 1)
         for i in range(8):
+            part = slice(8 * i, 8 * i + 8)
             rows = slice(64 * chunk + 8 * i, 64 * chunk + 8 * i + 8)
-            intensity, grow, add = rates(work[0, rows, :], work[1, rows, :], densx[rows, :])
+            work[0, rows, :] = re[part]
+            work[1, rows, :] = im[part]
+            intensity, grow, add = rates(re[part], im[part], densx[rows, :])
             for bit in (1, 2, 4):
                 there = group >= bit
                 grow2, add2 = roll(grow, 16 * bit, 1), roll(add, 16 * bit, 1)
@@ -433,6 +445,12 @@
                 jnp.where(group == i, roll(v, 16 * (i + 1), 1), old)
                 for v, old in zip((grow, add), maps)
             ]
+        if chunk == 0:
+
+            @pl.when(g < GROUP - 1)
+            def _():
+                pl.semaphore_wait(ready, GROUP - 1 - g)
+
         send2[chunk, 0] = maps[0]
         send2[chunk, 1] = maps[1]
         send_map(send2, recv2, 0, chunk)
@@ -488,14 +506,14 @@
             re, im = fields[a]
             sende[i, a, 0] = re
             sende[i, a, 1] = im
-            _, decays, source = rates(re, im, densy[:, LANES * a : LANES * (a + 1)])
-            dec[i, a] = decays
-            src[i, a] = source
+            _, decays, source = rates(re, im, densy[s, :, LANES * a : LANES * (a + 1)])
             pairs.append((decays * flip(decays), decays * flip(source) + source))
         for h in range(4):
             even, odd = pairs[2 * h], pairs[2 * h + 1]
             grow = jnp.where(top, even[0], odd[0])
             add = jnp.where(top, flip(even[1]), odd[1])
+            pairmap[i, h, 0] = grow
+            pairmap[i, h, 1] = add
             if maps[h] is not None:
                 grow, add = grow * maps[h][0], grow * maps[h][1] + add
             maps[h] = (grow, add)
@@ -508,32 +526,37 @@
     recve[s] = sende[s]
 
     enter(recv5, 1, ent5)
-    current = []
-    for h in range(4):
-        v = ent5[h]
-        turned = flip(v)
-        current += [jnp.where(top, v, turned), jnp.where(top, turned, v)]
-    for i in range(4):
-        for a in range(RADIX):
-            decays, source = dec[i, a], src[i, a]
-            first = decays * current[a] + source
-            electrons = decays * jnp.where(top, current[a], flip(first)) + source
-            send6[i, a] = electrons
-            current[a] = jnp.where(top, flip(electrons), electrons)
+    for i in range(GROUP):
+        for h in range(4):
+            if i == 0:
+                send6[0, h] = ent5[h]
+            else:
+                send6[i, h] = pairmap[i - 1, h, 0] * send6[i - 1, h] + pairmap[i - 1, h, 1]
         send_own(send6, recv6, 1, i)
     recv6[s] = send6[s]
 
-    for k in range(GROUP):
-
-        @pl.when(k != s)
-        def _():
+    for step in range(GROUP):
+        k = lax.rem(s + step, GROUP)
+        if step:
             pltpu.make_async_copy(recve.at[k], recve.at[k], own_recv.at[0, k]).wait()
+        for a in range(RADIX):
+            intensity, decays, source = rates(
+                recve[k, a, 0], recve[k, a, 1], densy[k, :, LANES * a : LANES * (a + 1)]
+            )
+            inten[step, a] = KERR_COEF * intensity
+            dec[step, a] = jnp.where(top, decays, decays * flip(decays))
+            src[step, a] = jnp.where(top, source, decays * flip(source) + source)
+    for step in range(GROUP):
+        k = lax.rem(s + step, GROUP)
+        if step:
             pltpu.make_async_copy(recv6.at[k], recv6.at[k], own_recv.at[1, k]).wait()
-
         for a in range(RADIX):
-            re, im, electrons = recve[k, a, 0], recve[k, a, 1], recv6[k, a]
-            intensity = re * re + im * im
-            sin, cos = sincos(KERR_COEF * intensity - PLASMA * electrons)
+            packed = recv6[k, a // 2]
+            turned = flip(packed)
+            pair = (packed, turned) if a % 2 == 0 else (turned, packed)
+            electrons = dec[step, a] * jnp.where(top, *pair) + src[step, a]
+            sin, cos = sincos(inten[step, a] - PLASMA * electrons)
+            re, im = recve[k, a, 0], recve[k, a, 1]
             new_re, new_im = re * cos - im * sin, re * sin + im * cos
             for t in range(2):
                 rows = pl.ds(64 * k + 2 * a + t, 4, stride=16)
@@ -572,6 +595,7 @@
     chunks = vmem(4, 2, 8, LANES)
     incoming = vmem(GROUP - 1, 4, 2, 8, LANES)
     tall = vmem(4, RADIX, 8, LANES)
+    short = vmem(4, 4, 8, LANES)
     fields = vmem(4, RADIX, 2, 8, LANES)
     plane = vmem(NX, LANES)
     out, ele = pl.pallas_call(
@@ -586,13 +610,14 @@
             vmem(2, NX, LANES), plane, vmem(16, NY), vmem(1, NX), vmem(8, LANES),
             vmem(NX, 2 * NX), vmem(NX, NX), vmem(NX, NX), vmem(2, 8, LANES), vmem(LANES, LANES),
             vmem(NX, NX), vmem(2 * NX, NX), vmem(2 * NX, NX), vmem(2 * NX, NX),
-            vmem(2, 8, LANES), plane, vmem(8, NY),
+            vmem(2, 8, LANES), plane, vmem(GROUP, 8, NY),
             pltpu.VMEM((3, 2 * NX, NX), jnp.bfloat16),
             pltpu.VMEM((2, 2 * NX, NX), jnp.bfloat16),
             pltpu.VMEM((2, 2, NX, NX), jnp.bfloat16),
             team, team, vmem(2, NX, LANES), plane, plane,
             chunks, incoming, vmem(4, 8, LANES), team, team, fields, tall, tall, tall,
-            fields, fields, chunks, incoming, vmem(4, 8, LANES), tall, tall,
+            fields, fields, chunks, incoming, vmem(4, 8, LANES), short, short,
+            vmem(4, 4, 2, 8, LANES),
             pltpu.SemaphoreType.DMA((10,)),
             pltpu.SemaphoreType.REGULAR,
             pltpu.SemaphoreType.DMA((2,)),

time: 34.1 us -> 33.1 us (0.971)
  Pallas kernels: 33.4 us -> 32.2 us
    pallas_call x1, Pallas kernels: 32.6 us -> 31.5 us  [local(): pl.pallas_call(kernel, out_shape=(jax.ShapeDtypeStruct((2, NX, LANES), F3...]
where the time goes in v6:
time: 33.1 us; the launch traced here: 32.9 us
  Pallas kernels  32.2 us (97%)
  between operations  0.64 us (2%)
    pallas_call x1, Pallas kernels, local(): pl.pallas_call(kernel, out_shape=(jax.ShapeDtypeStruct((2, NX, LANES), F3...  31.5 us
    pallas_call x1, Pallas kernels, local(): pl.pallas_call(finish, out_shape=(jax.ShapeDtypeStruct((2, NX, LANES), F3...  0.76 us

profile of v6, /device:TPU:1, one launch (start us, length us, event | category | flops | bytes accessed | tf_op | source)
XLA Modules:
  0.0 32.9 jit_solution(7102318362878410647)
XLA Ops:
  0.6 31.5 %split_step.1 = (f32[2,256,128]{2,1,0:T(8,128)S(1)}, f32[256,128]{1,0:T(8,128)S(1)}) custom-call(f32[2,256,128]{2,1,0:T(8,128)} %bitcast.17, f32[256,1024]{1,0:T(8,128)} %dens_hbm.1, f32[1,256]{1,0:T(1,128)} %bitcast.19, f32[8,128]{1,0:T(8,128)} %bitcast.18, f32[256,512]{1,0:T(8,128)} %constant.10.clone.tx_hbm, f32[256,256]{1,0:T(8,128)} %constant.11.clone.wf_hbm, ...), custom_call_target="tpu_custom_call" | custom-call | tf_op jit(solution)/shard_map/split_step/pallas_call | solution.py:601
  32.1 0.8 %finish.1 = (f32[2,256,128]{2,1,0:T(8,128)}, f32[256,128]{1,0:T(8,128)}) custom-call(f32[2,256,128]{2,1,0:T(8,128)S(1)} %get-tuple-element.6.a, f32[256,128]{1,0:T(8,128)S(1)} %get-tuple-element.7.b), custom_call_target="tpu_custom_call" | custom-call | tf_op jit(solution)/shard_map/finish/pallas_call | solution.py:642

commit v7 on v6

--- a/solution.py
+++ b/solution.py
@@ -276,9 +276,9 @@
                 for chunk in range(4):
                     total[chunk] = dst_ref[k, chunk, 0] * total[chunk] + dst_ref[k, chunk, 1]
 
-    def send_own(src_ref, dst_ref, phase, i):
-        @pl.when(i != s)
-        def _():
+    def send_own(src_ref, dst_ref, phase):
+        for dz, dc in ((1, 1), (1, 0), (0, 1)):
+            i = zs[dz] + cs[dc]
             pltpu.make_async_remote_copy(
                 src_ref=src_ref.at[i],
                 dst_ref=dst_ref.at[s],
@@ -521,8 +521,7 @@
         send5[h, 0] = maps[h][0]
         send5[h, 1] = maps[h][1]
         send_map(send5, recv5, 1, h)
-    for i in range(GROUP):
-        send_own(sende, recve, 0, i)
+    send_own(sende, recve, 0)
     recve[s] = sende[s]
 
     enter(recv5, 1, ent5)
@@ -532,7 +531,7 @@
                 send6[0, h] = ent5[h]
             else:
                 send6[i, h] = pairmap[i - 1, h, 0] * send6[i - 1, h] + pairmap[i - 1, h, 1]
-        send_own(send6, recv6, 1, i)
+    send_own(send6, recv6, 1)
     recv6[s] = send6[s]
 
     for step in range(GROUP):

time: 33.1 us -> 33 us (level)
  no operation moved by 1% of the time
where the time goes in v7:
time: 33 us; the launch traced here: 32.7 us
  Pallas kernels  32.1 us (97%)
  between operations  0.64 us (2%)
    pallas_call x1, Pallas kernels, local(): pl.pallas_call(kernel, out_shape=(jax.ShapeDtypeStruct((2, NX, LANES), F3...  31.3 us
    pallas_call x1, Pallas kernels, local(): pl.pallas_call(finish, out_shape=(jax.ShapeDtypeStruct((2, NX, LANES), F3...  0.76 us

profile of v7, /device:TPU:1, one launch (start us, length us, event | category | flops | bytes accessed | tf_op | source)
XLA Modules:
  0.0 32.7 jit_solution(15601397130160408296)
XLA Ops:
  0.6 31.3 %split_step.1 = (f32[2,256,128]{2,1,0:T(8,128)S(1)}, f32[256,128]{1,0:T(8,128)S(1)}) custom-call(f32[2,256,128]{2,1,0:T(8,128)} %bitcast.17, f32[256,1024]{1,0:T(8,128)} %dens_hbm.1, f32[1,256]{1,0:T(1,128)} %bitcast.19, f32[8,128]{1,0:T(8,128)} %bitcast.18, f32[256,512]{1,0:T(8,128)} %constant.10.clone.tx_hbm, f32[256,256]{1,0:T(8,128)} %constant.11.clone.wf_hbm, ...), custom_call_target="tpu_custom_call" | custom-call | tf_op jit(solution)/shard_map/split_step/pallas_call | solution.py:600
  31.9 0.8 %finish.1 = (f32[2,256,128]{2,1,0:T(8,128)}, f32[256,128]{1,0:T(8,128)}) custom-call(f32[2,256,128]{2,1,0:T(8,128)S(1)} %get-tuple-element.6.a, f32[256,128]{1,0:T(8,128)S(1)} %get-tuple-element.7.b), custom_call_target="tpu_custom_call" | custom-call | tf_op jit(solution)/shard_map/finish/pallas_call | solution.py:641

commit v8 on v7

--- a/solution.py
+++ b/solution.py
@@ -524,17 +524,7 @@
     send_own(sende, recve, 0)
     recve[s] = sende[s]
 
-    enter(recv5, 1, ent5)
-    for i in range(GROUP):
-        for h in range(4):
-            if i == 0:
-                send6[0, h] = ent5[h]
-            else:
-                send6[i, h] = pairmap[i - 1, h, 0] * send6[i - 1, h] + pairmap[i - 1, h, 1]
-    send_own(send6, recv6, 1)
-    recv6[s] = send6[s]
-
-    for step in range(GROUP):
+    def own_rates(step):
         k = lax.rem(s + step, GROUP)
         if step:
             pltpu.make_async_copy(recve.at[k], recve.at[k], own_recv.at[0, k]).wait()
@@ -545,6 +535,20 @@
             inten[step, a] = KERR_COEF * intensity
             dec[step, a] = jnp.where(top, decays, decays * flip(decays))
             src[step, a] = jnp.where(top, source, decays * flip(source) + source)
+
+    own_rates(0)
+    enter(recv5, 1, ent5)
+    for i in range(GROUP):
+        for h in range(4):
+            if i == 0:
+                send6[0, h] = ent5[h]
+            else:
+                send6[i, h] = pairmap[i - 1, h, 0] * send6[i - 1, h] + pairmap[i - 1, h, 1]
+    send_own(send6, recv6, 1)
+    recv6[s] = send6[s]
+
+    for step in range(1, GROUP):
+        own_rates(step)
     for step in range(GROUP):
         k = lax.rem(s + step, GROUP)
         if step:

time: 33 us -> 33 us (level)
  no operation moved by 1% of the time
where the time goes in v8:
time: 33 us; the launch traced here: 32.7 us
  Pallas kernels  32.1 us (97%)
  between operations  0.64 us (2%)
    pallas_call x1, Pallas kernels, local(): pl.pallas_call(kernel, out_shape=(jax.ShapeDtypeStruct((2, NX, LANES), F3...  31.3 us
    pallas_call x1, Pallas kernels, local(): pl.pallas_call(finish, out_shape=(jax.ShapeDtypeStruct((2, NX, LANES), F3...  0.76 us

profile of v8, /device:TPU:1, one launch (start us, length us, event | category | flops | bytes accessed | tf_op | source)
XLA Modules:
  0.0 32.7 jit_solution(6299229192819943777)
XLA Ops:
  0.6 31.3 %split_step.1 = (f32[2,256,128]{2,1,0:T(8,128)S(1)}, f32[256,128]{1,0:T(8,128)S(1)}) custom-call(f32[2,256,128]{2,1,0:T(8,128)} %bitcast.17, f32[256,1024]{1,0:T(8,128)} %dens_hbm.1, f32[1,256]{1,0:T(1,128)} %bitcast.19, f32[8,128]{1,0:T(8,128)} %bitcast.18, f32[256,512]{1,0:T(8,128)} %constant.10.clone.tx_hbm, f32[256,256]{1,0:T(8,128)} %constant.11.clone.wf_hbm, ...), custom_call_target="tpu_custom_call" | custom-call | tf_op jit(solution)/shard_map/split_step/pallas_call | solution.py:604
  31.9 0.8 %finish.1 = (f32[2,256,128]{2,1,0:T(8,128)}, f32[256,128]{1,0:T(8,128)}) custom-call(f32[2,256,128]{2,1,0:T(8,128)S(1)} %get-tuple-element.6.a, f32[256,128]{1,0:T(8,128)S(1)} %get-tuple-element.7.b), custom_call_target="tpu_custom_call" | custom-call | tf_op jit(solution)/shard_map/finish/pallas_call | solution.py:645
